TPU v7x, 32 devices: a whole 2x2x4 slice. The times are simulated.
32 devices in a mesh: dp: 4 (over z), space: 2 (over core), mp: 4 (over y, x).
Axes of the slice: x: 2, y: 2, z: 4, core: 2. Of those that a mesh axis runs over, the one named last changes fastest.
Arguments:
- features: bfloat16 [64, 64, 1024], P(('dp', 'space'), None, 'mp'), parts along dimension 0, may hold values from -6 to 6
- deconv_weight: bfloat16 [4, 512, 1024], P(None, 'mp'), may hold values from -0.1875 to 0.1875
- deconv_bias: float32 [512], P('mp'), may hold values from -3 to 3
- lateral_eight: bfloat16 [256, 512], P('mp'), may hold values from -0.25 to 0.25
- lateral_coarse: bfloat16 [2, 256, 1024], P(None, 'mp'), may hold values from -0.1875 to 0.1875
- output_conv: bfloat16 [3, 256, 9, 256], P(None, 'mp'), may hold values from -0.125 to 0.125
- norm_gain: float32 [6, 256], replicated, may hold values from 0.1 to 1.9
- norm_shift: float32 [6, 256], replicated, may hold values from -3 to 3
Outputs:
- level_eight: bfloat16 [256, 16384], P('mp', ('dp', 'space')), parts along dimension 1
- level_sixteen: bfloat16 [256, 4096], P('mp', ('dp', 'space')), parts along dimension 1
- level_thirty: bfloat16 [256, 1024], P('mp', ('dp', 'space')), parts along dimension 1
- level_sixty: bfloat16 [256, 256], P('mp', ('dp', 'space')), parts along dimension 1
There are 4 independent parts, one for each index of `dp`. A program takes and returns all parts, laid end to end along the dimension named above; an argument that names none is the same for every part. Nothing has to cross between parts.
All inputs are finite; a program needn't handle non-finite values.
Results may differ from a plain program's by a relative error of at most 0.015.
Values may be sent and summed in bfloat16 or wider, within the bound.
A program may use at most 64 MiB of HBM per device.

v0:
```python
import jax
import jax.numpy as jnp
from jax import lax
from jax.sharding import PartitionSpec as P

EPSILON = 1e-06


def extended(block, sides, width):
    for axis, dim in sides:
        count = lax.axis_size(axis)
        forward = [(i, i + 1) for i in range(count - 1)]
        backward = [(target, source) for source, target in forward]
        low = lax.ppermute(
            lax.slice_in_dim(block, block.shape[dim] - width, None, axis=dim), axis, forward
        )
        high = lax.ppermute(lax.slice_in_dim(block, 0, width, axis=dim), axis, backward)
        block = jnp.concatenate([low, block, high], axis=dim)
    return block


def pool_pairs(values):
    height, width, depth = values.shape
    return jnp.max(values.reshape(height // 2, 2, width // 2, 2, depth), axis=(1, 3))


def contract_last(weight_rows, data):
    return lax.dot_general(
        weight_rows, data, (((1,), (1,)), ((), ())), preferred_element_type=jnp.float32
    )


def apply_norm(values, sums, squares, neck_width, gain_row, shift_row):
    floats = values.astype(jnp.float32)
    center = (sums / neck_width)[None, :]
    spread = (squares / neck_width)[None, :] - center * center
    scaled = (floats - center) * lax.rsqrt(spread + EPSILON)
    return (scaled * gain_row[:, None] + shift_row[:, None]).astype(jnp.bfloat16)


def cell_moments(values):
    floats = values.astype(jnp.float32)
    return (jnp.sum(floats, axis=0), jnp.sum(floats * floats, axis=0))


def conv_taps(totals, padded, weight, height, width):
    depth = padded.shape[0]
    for tap_index in range(9):
        row_off = tap_index // 3
        col_off = tap_index % 3
        window = padded[:, row_off : row_off + height, col_off : col_off + width].reshape(
            depth, height * width
        )
        rows_used = weight[:, tap_index, :]
        totals = totals + jnp.dot(rows_used, window, preferred_element_type=jnp.float32)
    return totals


def pyramid_level(lateral, height, width, level_index, output_conv, norm_gain, norm_shift):
    local_ch = lateral.shape[0]
    neck_width = local_ch * lax.axis_size("mp")
    own_first = lax.axis_index("mp") * local_ch
    weight = output_conv[level_index]
    initial = jnp.zeros((local_ch, height * width), jnp.float32)
    gathered = lax.all_gather(lateral, "mp", axis=0, tiled=True)
    sums, squares = cell_moments(gathered)
    normed = apply_norm(
        gathered, sums, squares, neck_width, norm_gain[2 * level_index], norm_shift[2 * level_index]
    )
    rimmed = extended(normed.reshape(neck_width, height, width), (("space", 1),), 1)
    padded = jnp.pad(rimmed, ((0, 0), (0, 0), (1, 1)))
    conv_out = conv_taps(initial, padded, weight, height, width)
    convolved = conv_out.astype(jnp.bfloat16)
    sums, squares = lax.psum(cell_moments(convolved), "mp")
    gain_row = lax.dynamic_slice_in_dim(norm_gain[2 * level_index + 1], own_first, local_ch, 0)
    shift_row = lax.dynamic_slice_in_dim(norm_shift[2 * level_index + 1], own_first, local_ch, 0)
    return apply_norm(convolved, sums, squares, neck_width, gain_row, shift_row)


def channel_pyramid(
    features,
    deconv_weight,
    deconv_bias,
    lateral_eight,
    lateral_coarse,
    output_conv,
    norm_gain,
    norm_shift,
):
    row_count, col_count, _ = features.shape
    half_local = deconv_weight.shape[1]
    neck_local = lateral_coarse.shape[1]
    pixels = row_count * col_count
    coarse_pixels = row_count // 2 * (col_count // 2)
    deconv_flat = deconv_weight.reshape(4 * half_local, deconv_weight.shape[2])
    piece = lax.all_gather(features, "mp", axis=2, tiled=True)
    depth = piece.shape[2]
    flattened = piece.reshape(pixels, depth)
    raised = contract_last(deconv_flat, flattened)
    middle = contract_last(lateral_coarse[0], flattened)
    pooled_flat = pool_pairs(piece).reshape(coarse_pixels, depth)
    coarse = contract_last(lateral_coarse[1], pooled_flat)
    raised, middle, coarse = (raised, middle, coarse)
    raised = (
        raised.reshape(2, 2, half_local, row_count, col_count)
        + deconv_bias[None, None, :, None, None]
    )
    upsampled = raised.transpose(2, 3, 0, 4, 1).reshape(half_local, 4 * pixels).astype(jnp.bfloat16)
    piece = lax.all_gather(upsampled, "mp", axis=0, tiled=True)
    lateral_sum = jnp.dot(lateral_eight, piece, preferred_element_type=jnp.float32)
    lat_eight = lateral_sum.astype(jnp.bfloat16)
    lat_sixteen = middle.astype(jnp.bfloat16)
    lat_thirty = coarse.astype(jnp.bfloat16)
    level_eight = pyramid_level(
        lat_eight, 2 * row_count, 2 * col_count, 0, output_conv, norm_gain, norm_shift
    )
    level_sixteen = pyramid_level(
        lat_sixteen, row_count, col_count, 1, output_conv, norm_gain, norm_shift
    )
    level_thirty = pyramid_level(
        lat_thirty, row_count // 2, col_count // 2, 2, output_conv, norm_gain, norm_shift
    )
    level_sixty = level_thirty.reshape(neck_local, row_count // 2, col_count // 2)[
        :, ::2, ::2
    ].reshape(neck_local, -1)
    return (level_eight, level_sixteen, level_thirty, level_sixty)


def per_device(
    features,
    deconv_weight,
    deconv_bias,
    lateral_eight,
    lateral_coarse,
    output_conv,
    norm_gain,
    norm_shift,
):
    return channel_pyramid(
        features,
        deconv_weight,
        deconv_bias,
        lateral_eight,
        lateral_coarse,
        output_conv,
        norm_gain,
        norm_shift,
    )


def solution(mesh):
    return jax.shard_map(
        per_device,
        mesh=mesh,
        in_specs=(
            P(("dp", "space"), None, "mp"),
            P(None, "mp", None),
            P("mp"),
            P("mp", None),
            P(None, "mp", None),
            P(None, "mp", None, None),
            P(),
            P(),
        ),
        out_specs=(
            P("mp", ("dp", "space")),
            P("mp", ("dp", "space")),
            P("mp", ("dp", "space")),
            P("mp", ("dp", "space")),
        ),
        check_vma=False,
    )
```

profile of v0, /device:TPU:0, one launch (start us, length us, event | category | flops | bytes accessed | tf_op | source)
XLA Modules:
  0.0 179.7 jit_solution(12206708031647192003)
XLA Ops:
  7.2 0.7 all-gather.4.cloned.1.call-update
  8.0 0.9 fusion.99
  8.9 0.9 fusion.100
  9.8 0.7 fusion.86
  10.5 0.6 fusion.83
  11.1 0.7 fusion.82
  11.7 2.0 %slice_bitcast_fusion = (bf16[64,9,256]{2,0,1:T(8,128)(2,1)S(1)}, bf16[64,9,256]{2,0,1:T(8,128)(2,1)}, bf16[64,9,256]{2,0,1:T(8,128)(2,1)}) fusion(bf16[3,64,9,256]{3,1,2,0:T(8,128)(2,1)} %param.13), kind=kLoop, calls=%fused_computation.94 | loop fusion | bytes 1769472 | tf_op jit(solution)/shard_map/squeeze | solution.py:63
  13.8 25.2 %all-gather.4.cloned.1.call-done = bf16[8,64,1024]{2,1,0:T(8,128)(2,1)} async-done(((bf16[8,64,256]{2,1,0:T(8,128)(2,1)}), bf16[8,64,1024]{2,1,0:T(8,128)(2,1)}) %all-gather.4.cloned.1.call-update) | async-done | bytes 1048592 | tf_op jit(solution)/shard_map/all_gather | solution.py:96
  39.0 1.6 reshape.228
  40.5 2.5 %reduce_max.9 = bf16[4,32,1024]{2,1,0:T(8,128)(2,1)} reduce(bf16[4,2,32,2,1024]{4,3,2,1,0:T(2,128)(2,1)S(1)} %reshape.228, bf16[]{:T(256)} %constant.41.clone.1), dimensions={1,3}, to_apply=%region_12.13 | reduce | flops 393216 | bytes 1310722 | tf_op jit(solution)/shard_map/reduce_max | solution.py:24
  43.1 1.2 fusion.26
  44.3 8.2 %all_gather.19 = bf16[256,128]{1,0:T(8,128)(2,1)S(1)} all-gather(bf16[64,128]{1,0:T(8,128)(2,1)S(1)} %fusion.26), channel_id=1, replica_groups=mesh['dp'=4,'space'=2,'mp'=4] {'mp'}, dimensions={0}, use_global_device_ids=true | all-gather | bytes 81920 | tf_op jit(solution)/shard_map/all_gather | solution.py:65
  52.8 1.3 collective-permute-start.4
  54.1 1.3 collective-permute-start.5
  55.4 1.3 convolution_convert_fusion.1
  56.8 8.3 %all_gather.18 = bf16[256,512]{1,0:T(8,128)(2,1)S(1)} all-gather(bf16[64,512]{1,0:T(8,128)(2,1)S(1)} %convolution_convert_fusion.1), channel_id=1, replica_groups=mesh['dp'=4,'space'=2,'mp'=4] {'mp'}, dimensions={0}, use_global_device_ids=true | all-gather | bytes 327680 | tf_op jit(solution)/shard_map/all_gather | solution.py:65
  65.5 0.6 fusion.96
  66.1 1.4 collective-permute-start.2
  67.6 1.3 collective-permute-start.3
  68.9 0.7 fusion.15
  69.7 1.3 copy.13
  72.5 0.7 fusion.92
  73.7 33.4 %all-gather.6.cloned.1.call-done = bf16[512,2048]{0,1:T(8,128)(2,1)} async-done(((bf16[128,2048]{0,1:T(8,128)(2,1)}), bf16[512,2048]{0,1:T(8,128)(2,1)}) %all-gather.6.cloned.1.call-update) | async-done | bytes 2097168 | tf_op jit(solution)/shard_map/all_gather | solution.py:109
  107.1 3.0 %fusion.8 = bf16[64,2048]{1,0:T(8,128)(2,1)} fusion(bf16[512,2048]{0,1:T(8,128)(2,1)} %all-gather.6.cloned.1.call-done, bf16[64,512]{1,0:T(8,128)(2,1)S(1)} %copy-done.5), kind=kOutput, calls=%fused_computation.22 | convolution fusion | flops 134348800 | bytes 2424832 | tf_op jit(solution)/shard_map/dot_general | solution.py:110
  111.7 25.2 %all-gather.8.cloned.1.call-done = bf16[256,2048]{1,0:T(8,128)(2,1)} async-done(((bf16[64,2048]{1,0:T(8,128)(2,1)}), bf16[256,2048]{1,0:T(8,128)(2,1)}) %all-gather.8.cloned.1.call-update) | async-done | bytes 1048592 | tf_op jit(solution)/shard_map/all_gather | solution.py:65
  136.8 1.5 convert_reduce_fusion
  138.4 1.7 fusion.89
  140.5 1.6 collective-permute-start
  142.1 1.5 collective-permute-start.1
  143.6 0.2 fusion.91
  143.8 1.5 collective-permute-done.1
  145.4 2.9 %fusion.5 = bf16[256,18,130]{2,1,0:T(8,128)(2,1)S(1)} fusion(bf16[256,1,128]{2,1,0:T(2,128)(2,1)S(1)} %collective-permute-done.1, bf16[256,16,128]{2,1,0:T(8,128)(2,1)S(1)} %bitcast.224, bf16[256,1,128]{2,1,0:T(2,128)(2,1)S(1)} %collective-permute-done), kind=kLoop, calls=%fused_computation.7 | loop fusion | flops 7188480 | bytes 2377728 | tf_op jit(solution)/shard_map/concatenate | solution.py:18
  148.3 2.2 %fusion.93 = (bf16[256,16,128]{2,1,0:T(8,128)(2,1)S(1)}, bf16[256,16,128]{2,1,0:T(8,128)(2,1)S(1)}, bf16[256,16,128]{2,1,0:T(8,128)(2,1)S(1)}, bf16[256,16,128]{...) fusion(bf16[256,18,130]{2,1,0:T(8,128)(2,1)S(1)} %fusion.5), kind=kLoop, calls=%fused_computation.189 | loop fusion | bytes 12582912 | tf_op jit(solution)/shard_map/slice | solution.py:51
  150.5 0.3 fusion.41
  150.8 1.1 pad_maximum_fusion
  151.9 0.3 convolution_add_fusion.7
  152.2 0.3 convolution_add_fusion.6
  152.5 0.3 convolution_add_fusion.5
  152.8 0.6 copy-done.1
  153.4 0.6 convolution_add_fusion.4
  154.0 0.3 convolution_add_fusion.3
  154.3 0.3 convolution_add_fusion.2
  154.7 0.3 convolution_add_fusion.1
  155.0 0.3 fusion.90
  155.3 15.3 %all-reduce.3 = (f32[2048]{0:T(1024)S(1)}, f32[2048]{0:T(1024)S(1)}, f32[512]{0:T(512)S(1)}, f32[512]{0:T(512)S(1)}, f32[128]{0:T(128)S(1)}, /*index=5*/f32[128]{0:T(128)S(1)}) all-reduce(f32[2048]{0:T(1024)S(1)} %get-tuple-element.7, f32[2048]{0:T(1024)S(1)} %get-tuple-element.6, ...), channel_id=1, replica_groups=mesh['dp'=4,'space'=2,'mp'=4] {'mp'}, use_global_device_ids=true, to_apply=%region_5.6 | all-reduce | flops 5376 | bytes 43008 | tf_op jit(solution)/shard_map/psum | solution.py:74
  170.9 0.7 slice.317
  171.6 0.7 fusion.72
  172.3 0.8 fusion.56
  (76 shorter events, 4.8 us)
Async XLA Ops:
  7.2 61.7 %copy-start = (bf16[4,128,1024]{2,1,0:T(8,128)(2,1)S(1)}, bf16[4,128,1024]{2,1,0:T(8,128)(2,1)}, u32[]{:S(2)}) copy-start(bf16[4,128,1024]{2,1,0:T(8,128)(2,1)} %param.9) | copy-start | bytes 3145732
  7.2 31.8 %all-gather.4.cloned.1.call-start = ((), (), s32[]{:S(2)}) async-start(), calls=%async_computation | async-start | bytes 1310720 | tf_op jit(solution)/shard_map/all_gather | solution.py:96
  7.9 99.2 %all-gather.6.cloned.1.call-start = ((), (), s32[]{:S(2)}) async-start(), calls=%async_computation.1 | async-start | bytes 2621440 | tf_op jit(solution)/shard_map/all_gather | solution.py:109
  39.0 16.5 %copy-start.2 = (bf16[8,64,1024]{2,1,0:T(8,128)(2,1)S(1)}, bf16[8,64,1024]{2,1,0:T(8,128)(2,1)}, u32[]{:S(2)}) copy-start(bf16[8,64,1024]{2,1,0:T(8,128)(2,1)} %all-gather.4.cloned.1.call-done) | copy-start | bytes 3145732
  43.1 25.9 %copy-start.13 = (f32[128]{0:T(128)S(1)}, f32[128]{0:T(128)}, u32[]{:S(2)}) copy-start(f32[128]{0:T(128)} %param.10) | copy-start | bytes 1540
  52.8 18.3 %collective-permute-start.4 = (bf16[256,1,32]{0,2,1:T(8,128)(2,1)S(1)}, bf16[256,1,32]{0,2,1:T(8,128)(2,1)S(1)}, u32[]{:S(2)}, u32[]{:S(2)}) collective-permute-start(bf16[256,1,32]{0,2,1:T(8,128)(2,1)S(1)} %get-tuple-element.53), channel_id=1, source_target_pairs={{0,4},{1,5},{2,6},{3,7},{8,12},{9,13},{10,14},{11,15},{16,20},{17,... | collective-permute-start | bytes 49160 | tf_op jit(solution)/shard_map/ppermute | solution.py:14
  54.1 17.0 %collective-permute-start.5 = (bf16[256,1,32]{0,2,1:T(8,128)(2,1)S(1)}, bf16[256,1,32]{0,2,1:T(8,128)(2,1)S(1)}, u32[]{:S(2)}, u32[]{:S(2)}) collective-permute-start(bf16[256,1,32]{0,2,1:T(8,128)(2,1)S(1)} %get-tuple-element.54), channel_id=1, source_target_pairs={{4,0},{5,1},{6,2},{7,3},{12,8},{13,9},{14,10},{15,11},{20,16},{21,... | collective-permute-start | bytes 49160 | tf_op jit(solution)/shard_map/ppermute | solution.py:17
  66.1 7.0 %collective-permute-start.2 = (bf16[256,1,64]{0,2,1:T(8,128)(2,1)}, bf16[256,1,64]{0,2,1:T(8,128)(2,1)S(1)}, u32[]{:S(2)}, u32[]{:S(2)}) collective-permute-start(bf16[256,1,64]{0,2,1:T(8,128)(2,1)} %get-tuple-element.43), channel_id=1, source_target_pairs={{0,4},{1,5},{2,6},{3,7},{8,12},{9,13},{10,14},{11,15},{16,20},{17,... | collective-permute-start | bytes 98312 | tf_op jit(solution)/shard_map/ppermute | solution.py:14
  67.6 5.6 %collective-permute-start.3 = (bf16[256,1,64]{0,2,1:T(8,128)(2,1)}, bf16[256,1,64]{0,2,1:T(8,128)(2,1)S(1)}, u32[]{:S(2)}, u32[]{:S(2)}) collective-permute-start(bf16[256,1,64]{0,2,1:T(8,128)(2,1)} %get-tuple-element.44), channel_id=1, source_target_pairs={{4,0},{5,1},{6,2},{7,3},{12,8},{13,9},{14,10},{15,11},{20,16},{21,... | collective-permute-start | bytes 98312 | tf_op jit(solution)/shard_map/ppermute | solution.py:17
  71.0 65.8 %all-gather.8.cloned.1.call-start = ((), (), s32[]{:S(2)}) async-start(), calls=%async_computation.2 | async-start | bytes 1310720 | tf_op jit(solution)/shard_map/all_gather | solution.py:65
  72.3 1.2 copy-start.3
  73.1 34.0 %copy-start.5 = (bf16[64,512]{1,0:T(8,128)(2,1)S(1)}, bf16[64,512]{1,0:T(8,128)(2,1)}, u32[]{:S(2)}) copy-start(bf16[64,512]{1,0:T(8,128)(2,1)} %param.11) | copy-start | bytes 196612
  140.5 3.3 %collective-permute-start = (bf16[256,1,128]{2,1,0:T(2,128)(2,1)S(1)}, bf16[256,1,128]{2,1,0:T(2,128)(2,1)S(1)}, u32[]{:S(2)}, u32[]{:S(2)}) collective-permute-start(bf16[256,1,128]{2,1,0:T(2,128)(2,1)S(1)} %get-tuple-element.30), channel_id=1, source_target_pairs={{0,4},{1,5},{2,6},{3,7},{8,12},{9,13},{10,14},{11,15},{16,20},{17,... | collective-permute-start | bytes 196616 | tf_op jit(solution)/shard_map/ppermute | solution.py:14
  142.1 3.2 %collective-permute-start.1 = (bf16[256,1,128]{2,1,0:T(2,128)(2,1)S(1)}, bf16[256,1,128]{2,1,0:T(2,128)(2,1)S(1)}, u32[]{:S(2)}, u32[]{:S(2)}) collective-permute-start(bf16[256,1,128]{2,1,0:T(2,128)(2,1)S(1)} %get-tuple-element.31), channel_id=1, source_target_pairs={{4,0},{5,1},{6,2},{7,3},{12,8},{13,9},{14,10},{15,11},{20,16},{21,... | collective-permute-start | bytes 196616 | tf_op jit(solution)/shard_map/ppermute | solution.py:17
  148.3 2.2 %copy-start.4 = (bf16[64,9,256]{2,0,1:T(8,128)(2,1)S(1)}, bf16[64,9,256]{2,0,1:T(8,128)(2,1)}, u32[]{:S(2)}) copy-start(bf16[64,9,256]{2,0,1:T(8,128)(2,1)} %get-tuple-element.33) | copy-start | bytes 884740
  152.2 1.2 copy-start.1
  154.6 0.7 copy-start.11
  154.6 0.7 copy-start.12
  154.6 16.0 %copy-start.9 = (f32[64]{0:T(128)S(1)}, f32[64]{0:T(128)}, u32[]{:S(2)}) copy-start(f32[64]{0:T(128)} %get-tuple-element.86) | copy-start | bytes 772
  154.7 16.0 %copy-start.10 = (f32[64]{0:T(128)S(1)}, f32[64]{0:T(128)}, u32[]{:S(2)}) copy-start(f32[64]{0:T(128)} %get-tuple-element.87) | copy-start | bytes 772
  154.7 16.9 %copy-start.7 = (f32[64]{0:T(128)S(1)}, f32[64]{0:T(128)}, u32[]{:S(2)}) copy-start(f32[64]{0:T(128)} %get-tuple-element.83) | copy-start | bytes 772
  154.7 16.9 %copy-start.8 = (f32[64]{0:T(128)S(1)}, f32[64]{0:T(128)}, u32[]{:S(2)}) copy-start(f32[64]{0:T(128)} %get-tuple-element.85) | copy-start | bytes 772
  170.8 2.4 %copy-start.6 = (bf16[64,128]{1,0:T(8,128)(2,1)}, bf16[64,128]{1,0:T(8,128)(2,1)S(1)}, u32[]{:S(2)}) copy-start(bf16[64,128]{1,0:T(8,128)(2,1)S(1)} %fusion.81) | copy-start | bytes 49156
Sparse Core Ops, SparseCore 0:
  9.8 29.1 all-gather.3
  71.2 35.9 all-gather.5
  110.3 26.4 all-gather.7
where the time goes:
time: 180 us
  waiting for transfers between devices  86.1 us (48%)
  blocking collectives  31.9 us (18%)
  between operations  14.3 us (8%)
  local copies, waits for them, and re-layouts  13.9 us (8%)
  matrix products  13 us (7%)
  other arithmetic  12.1 us (7%)
  starting transfers between devices  8.49 us (5%)
    all_gather x1, waiting for transfers between devices, channel_pyramid(): piece = lax.all_gather(upsampled, 'mp', axis=0, tiled=True)  33.4 us
    all_gather x1, waiting for transfers between devices, channel_pyramid(): piece = lax.all_gather(features, 'mp', axis=2, tiled=True)  25.2 us
    all_gather x1, waiting for transfers between devices, pyramid_level(): gathered = lax.all_gather(lateral, 'mp', axis=0, tiled=True)  25.2 us
    all_gather x2, blocking collectives, pyramid_level(): gathered = lax.all_gather(lateral, 'mp', axis=0, tiled=True)  16.6 us
    psum x1, blocking collectives, pyramid_level(): sums, squares = lax.psum(cell_moments(convolved), 'mp')  15.3 us
    dot_general x27, matrix products, conv_taps(): jnp.dot(rows_used, window, preferred_element_type=jnp.float32)  6.68 us
    ppermute x3, starting transfers between devices, extended(): lax.ppermute(lax.slice_in_dim(block, block.shape[dim] - width, None, axis...  4.31 us
    concatenate x6, other arithmetic, extended(): block = jnp.concatenate([low, block, high], axis=dim)  4.2 us
  transfers between devices with their start and end apart: 9, of which 4 were waited for; matrix products, arithmetic and copies ran while one was open for 8% of the time, Pallas kernels for 0%

commit v1 on v0

--- a/solution.py
+++ b/solution.py
@@ -1,9 +1,26 @@
+import functools
 import jax
 import jax.numpy as jnp
 from jax import lax
 from jax.sharding import PartitionSpec as P
 
 EPSILON = 1e-06
+
+
+def guide_levels_all(x_local, axis_name, row_dim):
+    n_blocks = lax.axis_size(axis_name)
+    slots = tuple(((m, (m + 1) % n_blocks) for m in range(n_blocks)))
+    h_now = [None] * n_blocks
+    h_now[n_blocks - 1] = x_local
+    for num in range(n_blocks - 2, -1, -1):
+        h_now[num] = lax.ppermute(h_now[num + 1], perm=slots, axis_name=axis_name)
+    block_last = jnp.concatenate(h_now, axis=row_dim)
+    finding = lax.axis_index(axis_name)
+    ready = (finding + 1) * x_local.shape[row_dim]
+    return jnp.roll(block_last, ready, axis=row_dim)
+
+
+carry_outputs = functools.partial(guide_levels_all, axis_name="mp", row_dim=2)
 
 
 def extended(block, sides, width):
@@ -93,7 +110,7 @@
     pixels = row_count * col_count
     coarse_pixels = row_count // 2 * (col_count // 2)
     deconv_flat = deconv_weight.reshape(4 * half_local, deconv_weight.shape[2])
-    piece = lax.all_gather(features, "mp", axis=2, tiled=True)
+    piece = carry_outputs(features)
     depth = piece.shape[2]
     flattened = piece.reshape(pixels, depth)
     raised = contract_last(deconv_flat, flattened)

time: 180 us -> 151 us (0.84)
  waiting for transfers between devices: 86.1 us -> 45.5 us
  starting transfers between devices: 8.49 us -> 17 us
    all_gather x1, waiting for transfers between devices: 33.4 us -> 2.94 us  [channel_pyramid(): piece = lax.all_gather(upsampled, 'mp', axis=0, tiled=True)]
    all_gather x1 -> x0, waiting for transfers between devices: 25.2 us -> none  [channel_pyramid(): piece = lax.all_gather(features, 'mp', axis=2, tiled=True)]
    ppermute x0 -> x3, waiting for transfers between devices: none -> 16.8 us  [guide_levels_all(): h_now[num] = lax.ppermute(h_now[num + 1], perm=slots, axis_name=axis_name)]
    ppermute x3, starting transfers between devices: 4.31 us -> 9.28 us  [extended(): lax.ppermute(lax.slice_in_dim(block, block.shape[dim] - width, None, axis...]
    ppermute x0 -> x3, starting transfers between devices: none -> 3.81 us  [guide_levels_all(): h_now[num] = lax.ppermute(h_now[num + 1], perm=slots, axis_name=axis_name)]
    reshape x0 -> x1, local copies, waits for them, and re-layouts: none -> 2.86 us  [channel_pyramid(): raised.reshape(2, 2, half_local, row_count, col_count)]
  transfers between devices with their start and end apart: 9 -> 11, of which waited for: 4 -> 6; matrix products, arithmetic and copies ran while one was open for 8% -> 9% of each run, Pallas kernels for 0% -> 0%
where the time goes in v1:
time: 151 us
  waiting for transfers between devices  45.5 us (30%)
  blocking collectives  32.4 us (21%)
  starting transfers between devices  17 us (11%)
  local copies, waits for them, and re-layouts  15.3 us (10%)
  between operations  14.7 us (10%)
  matrix products  13 us (9%)
  other arithmetic  12.7 us (8%)
    all_gather x1, waiting for transfers between devices, pyramid_level(): gathered = lax.all_gather(lateral, 'mp', axis=0, tiled=True)  25.2 us
    all_gather x2, blocking collectives, pyramid_level(): gathered = lax.all_gather(lateral, 'mp', axis=0, tiled=True)  17.1 us
    ppermute x3, waiting for transfers between devices, guide_levels_all(): h_now[num] = lax.ppermute(h_now[num + 1], perm=slots, axis_name=axis_name)  16.8 us
    psum x1, blocking collectives, pyramid_level(): sums, squares = lax.psum(cell_moments(convolved), 'mp')  15.4 us
    ppermute x3, starting transfers between devices, extended(): lax.ppermute(lax.slice_in_dim(block, block.shape[dim] - width, None, axis...  9.28 us
    dot_general x27, matrix products, conv_taps(): jnp.dot(rows_used, window, preferred_element_type=jnp.float32)  6.68 us
    concatenate x6, other arithmetic, extended(): block = jnp.concatenate([low, block, high], axis=dim)  4.2 us
    ppermute x3, starting transfers between devices, extended(): lax.ppermute(lax.slice_in_dim(block, 0, width, axis=dim), axis, backward)  3.88 us
  transfers between devices with their start and end apart: 11, of which 6 were waited for; matrix products, arithmetic and copies ran while one was open for 9% of the time, Pallas kernels for 0%

profile of v1, /device:TPU:0, one launch (start us, length us, event | category | flops | bytes accessed | tf_op | source)
XLA Modules:
  0.0 150.7 jit_solution(5130454134014211410)
XLA Ops:
  7.2 3.0 %collective-permute-start = (bf16[8,64,256]{2,1,0:T(8,128)(2,1)}, bf16[8,64,256]{2,1,0:T(8,128)(2,1)S(1)}, u32[]{:S(2)}, u32[]{:S(2)}) collective-permute-start(bf16[8,64,256]{2,1,0:T(8,128)(2,1)} %param.8), channel_id=1, source_target_pairs={{0,1},{1,2},{2,3},{3,0},{4,5},{5,6},{6,7},{7,4},{8,9},{9,10},{10,1... | collective-permute-start | bytes 786440 | tf_op jit(solution)/shard_map/ppermute | solution.py:16
  10.3 0.9 fusion.100
  11.2 6.5 %collective-permute-done = bf16[8,64,256]{2,1,0:T(8,128)(2,1)S(1)} collective-permute-done((bf16[8,64,256]{2,1,0:T(8,128)(2,1)}, bf16[8,64,256]{2,1,0:T(8,128)(2,1)S(1)}, u32[]{:S(2)}, u32[]{:S(2)}) %collective-permute-start) | collective-permute-done | bytes 262176 | tf_op jit(solution)/shard_map/ppermute | solution.py:16
  17.7 0.8 collective-permute-start.1
  18.5 0.9 fusion.99
  19.4 0.6 fusion.83
  20.0 0.7 fusion.82
  20.7 5.4 %collective-permute-done.1 = bf16[8,64,256]{2,1,0:T(8,128)(2,1)S(1)} collective-permute-done((bf16[8,64,256]{2,1,0:T(8,128)(2,1)S(1)}, bf16[8,64,256]{2,1,0:T(8,128)(2,1)S(1)}, u32[]{:S(2)}, u32[]{:S(2)}) %collective-permute-start.1) | collective-permute-done | bytes 262176 | tf_op jit(solution)/shard_map/ppermute | solution.py:16
  26.1 0.7 fusion.86
  26.8 2.0 %slice_bitcast_fusion = (bf16[64,9,256]{2,0,1:T(8,128)(2,1)S(1)}, bf16[64,9,256]{2,0,1:T(8,128)(2,1)}, bf16[64,9,256]{2,0,1:T(8,128)(2,1)}) fusion(bf16[3,64,9,256]{3,1,2,0:T(8,128)(2,1)} %param.13), kind=kLoop, calls=%fused_computation.95 | loop fusion | bytes 1769472 | tf_op jit(solution)/shard_map/squeeze | solution.py:80
  28.8 4.8 %collective-permute-done.2 = bf16[8,64,256]{2,1,0:T(8,128)(2,1)S(1)} collective-permute-done((bf16[8,64,256]{2,1,0:T(8,128)(2,1)S(1)}, bf16[8,64,256]{2,1,0:T(8,128)(2,1)S(1)}, u32[]{:S(2)}, u32[]{:S(2)}) %collective-permute-start.2) | collective-permute-done | bytes 262176 | tf_op jit(solution)/shard_map/ppermute | solution.py:16
  34.0 0.4 reshape.230
  34.5 1.7 %convolution_bitcast_fusion = f32[512,512]{0,1:T(8,128)} fusion(bf16[512,1024]{1,0:T(8,128)(2,1)S(1)} %bitcast.224, bf16[512,1024]{1,0:T(8,128)(2,1)S(1)} %bitcast.220), kind=kOutput, calls=%fused_computation.28 | convolution fusion | flops 536870912 | bytes 3145728 | tf_op jit(solution)/shard_map/dot_general | solution.py:45
  36.2 2.9 %reshape.211 = f32[2,2,128,8,64]{2,1,0,4,3:T(2,128)} reshape(f32[512,512]{0,1:T(8,128)} %convolution_bitcast_fusion) | data formatting | bytes 2097152 | tf_op jit(solution)/shard_map/reshape | solution.py:122
  39.1 1.4 fusion.50
  40.4 1.4 copy.22
  41.9 1.3 fusion.19
  43.2 8.8 %all_gather.14 = bf16[256,512]{1,0:T(8,128)(2,1)S(1)} all-gather(bf16[64,512]{1,0:T(8,128)(2,1)S(1)} %fusion.19), channel_id=1, replica_groups=mesh['dp'=4,'space'=2,'mp'=4] {'mp'}, dimensions={0}, use_global_device_ids=true | all-gather | bytes 327680 | tf_op jit(solution)/shard_map/all_gather | solution.py:82
  52.4 1.8 %reduce_max.9 = bf16[4,32,1024]{2,1,0:T(8,128)(2,1)S(1)} reduce(bf16[4,2,32,2,1024]{4,3,2,1,0:T(2,128)(2,1)S(1)} %reshape.230, bf16[]{:T(256)} %constant.64.clone.1), dimensions={1,3}, to_apply=%region_12.13 | reduce | flops 393216 | bytes 1310722 | tf_op jit(solution)/shard_map/reduce_max | solution.py:41
  54.5 8.3 %all_gather.15 = bf16[256,128]{1,0:T(8,128)(2,1)S(1)} all-gather(bf16[64,128]{1,0:T(8,128)(2,1)S(1)} %fusion.25), channel_id=1, replica_groups=mesh['dp'=4,'space'=2,'mp'=4] {'mp'}, dimensions={0}, use_global_device_ids=true | all-gather | bytes 81920 | tf_op jit(solution)/shard_map/all_gather | solution.py:82
  63.1 1.3 collective-permute-start.8
  64.4 3.0 %collective-permute-start.7 = (bf16[256,1,32]{0,2,1:T(8,128)(2,1)S(1)}, bf16[256,1,32]{0,2,1:T(8,128)(2,1)S(1)}, u32[]{:S(2)}, u32[]{:S(2)}) collective-permute-start(bf16[256,1,32]{0,2,1:T(8,128)(2,1)S(1)} %get-tuple-element.53), channel_id=1, source_target_pairs={{0,4},{1,5},{2,6},{3,7},{8,12},{9,13},{10,14},{11,15},{16,20},{17,... | collective-permute-start | bytes 49160 | tf_op jit(solution)/shard_map/ppermute | solution.py:31
  67.4 1.3 collective-permute-start.6
  68.7 3.0 %collective-permute-start.5 = (bf16[256,1,64]{0,2,1:T(8,128)(2,1)S(1)}, bf16[256,1,64]{0,2,1:T(8,128)(2,1)S(1)}, u32[]{:S(2)}, u32[]{:S(2)}) collective-permute-start(bf16[256,1,64]{0,2,1:T(8,128)(2,1)S(1)} %get-tuple-element.43), channel_id=1, source_target_pairs={{0,4},{1,5},{2,6},{3,7},{8,12},{9,13},{10,14},{11,15},{16,20},{17,... | collective-permute-start | bytes 98312 | tf_op jit(solution)/shard_map/ppermute | solution.py:31
  73.1 0.7 fusion.92
  74.3 2.9 %all-gather.3.cloned.1.call-done = bf16[512,2048]{0,1:T(8,128)(2,1)} async-done(((bf16[128,2048]{0,1:T(8,128)(2,1)}), bf16[512,2048]{0,1:T(8,128)(2,1)}) %all-gather.3.cloned.1.call-update) | async-done | bytes 2097168 | tf_op jit(solution)/shard_map/all_gather | solution.py:126
  77.3 3.0 %fusion.8 = bf16[64,2048]{1,0:T(8,128)(2,1)} fusion(bf16[512,2048]{0,1:T(8,128)(2,1)} %all-gather.3.cloned.1.call-done, bf16[64,512]{1,0:T(8,128)(2,1)S(1)} %copy-done.6), kind=kOutput, calls=%fused_computation.22 | convolution fusion | flops 134348800 | bytes 2424832 | tf_op jit(solution)/shard_map/dot_general | solution.py:127
  81.8 25.2 %all-gather.5.cloned.1.call-done = bf16[256,2048]{1,0:T(8,128)(2,1)} async-done(((bf16[64,2048]{1,0:T(8,128)(2,1)}), bf16[256,2048]{1,0:T(8,128)(2,1)}) %all-gather.5.cloned.1.call-update) | async-done | bytes 1048592 | tf_op jit(solution)/shard_map/all_gather | solution.py:82
  107.0 1.5 %convert_reduce_fusion = (f32[2048]{0:T(1024)S(1)}, f32[2048]{0:T(1024)S(1)}) fusion(bf16[256,2048]{1,0:T(8,128)(2,1)} %all-gather.5.cloned.1.call-done), kind=kLoop, calls=%fused_computation.10 | loop fusion | flops 2093056 | bytes 1064960 | tf_op jit(solution)/shard_map/reduce_sum | solution.py:60
  108.5 1.7 %fusion.89 = bf16[32,8,16,128]{3,1,2,0:T(8,128)(2,1)S(1)} fusion(f32[256]{0:T(256)S(1)} %bitcast.260, f32[256]{0:T(256)S(1)} %bitcast.262, f32[2048]{0:T(1024)S(1)} %get-tuple-element.70, f32[2048]{0:T(1024)S(1)} %get-tuple-element.69, bf16[256,2048]{1,0:T(8,128)(2,1)} %all-gather.5.cloned.1.call-done), kind=kLoop, calls=%fused_computation.195 | loop fusion | flops 3145728 | bytes 2115584
  110.7 1.3 collective-permute-start.4
  112.0 3.2 %collective-permute-start.3 = (bf16[256,1,128]{2,1,0:T(2,128)(2,1)S(1)}, bf16[256,1,128]{2,1,0:T(2,128)(2,1)S(1)}, u32[]{:S(2)}, u32[]{:S(2)}) collective-permute-start(bf16[256,1,128]{2,1,0:T(2,128)(2,1)S(1)} %get-tuple-element.30), channel_id=1, source_target_pairs={{0,4},{1,5},{2,6},{3,7},{8,12},{9,13},{10,14},{11,15},{16,20},{17,... | collective-permute-start | bytes 196616 | tf_op jit(solution)/shard_map/ppermute | solution.py:31
  115.5 0.5 collective-permute-done.3
  116.0 2.9 %fusion.5 = bf16[256,18,130]{2,1,0:T(8,128)(2,1)S(1)} fusion(bf16[256,1,128]{2,1,0:T(2,128)(2,1)S(1)} %collective-permute-done.4, bf16[256,16,128]{2,1,0:T(8,128)(2,1)S(1)} %bitcast.222, bf16[256,1,128]{2,1,0:T(2,128)(2,1)S(1)} %collective-permute-done.3), kind=kLoop, calls=%fused_computation.7 | loop fusion | flops 7188480 | bytes 2377728 | tf_op jit(solution)/shard_map/concatenate | solution.py:35
  119.0 2.2 %fusion.93 = (bf16[256,16,128]{2,1,0:T(8,128)(2,1)S(1)}, bf16[256,16,128]{2,1,0:T(8,128)(2,1)S(1)}, bf16[256,16,128]{2,1,0:T(8,128)(2,1)S(1)}, bf16[256,16,128]{...) fusion(bf16[256,18,130]{2,1,0:T(8,128)(2,1)S(1)} %fusion.5), kind=kLoop, calls=%fused_computation.199 | loop fusion | bytes 12582912 | tf_op jit(solution)/shard_map/slice | solution.py:68
  121.5 1.1 pad_maximum_fusion
  122.5 0.3 convolution_add_fusion.7
  123.2 0.3 convolution_add_fusion.5
  123.5 0.6 copy-done.1
  124.1 0.6 convolution_add_fusion.4
  124.7 0.3 convolution_add_fusion.3
  125.0 0.3 convolution_add_fusion.2
  125.3 0.3 convolution_add_fusion.1
  125.6 0.3 fusion.90
  126.0 15.4 %all-reduce.3 = (f32[2048]{0:T(1024)S(1)}, f32[2048]{0:T(1024)S(1)}, f32[512]{0:T(512)S(1)}, f32[512]{0:T(512)S(1)}, f32[128]{0:T(128)S(1)}, /*index=5*/f32[128]{0:T(128)S(1)}) all-reduce(f32[2048]{0:T(1024)S(1)} %get-tuple-element.7, f32[2048]{0:T(1024)S(1)} %get-tuple-element.6, ...), channel_id=1, replica_groups=mesh['dp'=4,'space'=2,'mp'=4] {'mp'}, use_global_device_ids=true, to_apply=%region_5.6 | all-reduce | flops 5376 | bytes 43008 | tf_op jit(solution)/shard_map/psum | solution.py:91
  141.6 0.7 slice.317
  142.3 0.8 fusion.56
  143.1 0.7 fusion.72
  (92 shorter events, 6.2 us)
Async XLA Ops:
  7.2 27.3 %copy-start = (bf16[4,128,1024]{2,1,0:T(8,128)(2,1)S(1)}, bf16[4,128,1024]{2,1,0:T(8,128)(2,1)}, u32[]{:S(2)}) copy-start(bf16[4,128,1024]{2,1,0:T(8,128)(2,1)} %param.9) | copy-start | bytes 3145732
  7.2 26.5 %copy-start.4 = (bf16[8,64,256]{2,1,0:T(8,128)(2,1)S(1)}, bf16[8,64,256]{2,1,0:T(8,128)(2,1)}, u32[]{:S(2)}) copy-start(bf16[8,64,256]{2,1,0:T(8,128)(2,1)} %param.8) | copy-start | bytes 786436
  7.2 70.1 %all-gather.3.cloned.1.call-start = ((), (), s32[]{:S(2)}) async-start(), calls=%async_computation | async-start | bytes 2621440 | tf_op jit(solution)/shard_map/all_gather | solution.py:126
  7.2 10.5 %collective-permute-start = (bf16[8,64,256]{2,1,0:T(8,128)(2,1)}, bf16[8,64,256]{2,1,0:T(8,128)(2,1)S(1)}, u32[]{:S(2)}, u32[]{:S(2)}) collective-permute-start(bf16[8,64,256]{2,1,0:T(8,128)(2,1)} %param.8), channel_id=1, source_target_pairs={{0,1},{1,2},{2,3},{3,0},{4,5},{5,6},{6,7},{7,4},{8,9},{9,10},{10,1... | collective-permute-start | bytes 786440 | tf_op jit(solution)/shard_map/ppermute | solution.py:16
  17.7 8.4 %collective-permute-start.1 = (bf16[8,64,256]{2,1,0:T(8,128)(2,1)S(1)}, bf16[8,64,256]{2,1,0:T(8,128)(2,1)S(1)}, u32[]{:S(2)}, u32[]{:S(2)}) collective-permute-start(bf16[8,64,256]{2,1,0:T(8,128)(2,1)S(1)} %collective-permute-done), channel_id=1, source_target_pairs={{0,1},{1,2},{2,3},{3,0},{4,5},{5,6},{6,7},{7,4},{8,9},{9,10},{10,1... | collective-permute-start | bytes 786440 | tf_op jit(solution)/shard_map/ppermute | solution.py:16
  26.1 7.5 %collective-permute-start.2 = (bf16[8,64,256]{2,1,0:T(8,128)(2,1)S(1)}, bf16[8,64,256]{2,1,0:T(8,128)(2,1)S(1)}, u32[]{:S(2)}, u32[]{:S(2)}) collective-permute-start(bf16[8,64,256]{2,1,0:T(8,128)(2,1)S(1)} %collective-permute-done.1), channel_id=1, source_target_pairs={{0,1},{1,2},{2,3},{3,0},{4,5},{5,6},{6,7},{7,4},{8,9},{9,10},{10,1... | collective-permute-start | bytes 786440 | tf_op jit(solution)/shard_map/ppermute | solution.py:16
  34.5 4.6 %copy-start.14 = (f32[128]{0:T(128)S(1)}, f32[128]{0:T(128)}, u32[]{:S(2)}) copy-start(f32[128]{0:T(128)} %param.10) | copy-start | bytes 1540
  41.8 65.2 %all-gather.5.cloned.1.call-start = ((), (), s32[]{:S(2)}) async-start(), calls=%async_computation.1 | async-start | bytes 1310720 | tf_op jit(solution)/shard_map/all_gather | solution.py:82
  43.2 11.1 %copy-start.5 = (bf16[2,64,1024]{2,1,0:T(8,128)(2,1)S(1)}, bf16[2,64,1024]{2,1,0:T(8,128)(2,1)}, u32[]{:S(2)}) copy-start(bf16[2,64,1024]{2,1,0:T(8,128)(2,1)} %param.12) | copy-start | bytes 786436
  63.1 8.7 %collective-permute-start.8 = (bf16[256,1,32]{0,2,1:T(8,128)(2,1)S(1)}, bf16[256,1,32]{0,2,1:T(8,128)(2,1)S(1)}, u32[]{:S(2)}, u32[]{:S(2)}) collective-permute-start(bf16[256,1,32]{0,2,1:T(8,128)(2,1)S(1)} %get-tuple-element.54), channel_id=1, source_target_pairs={{4,0},{5,1},{6,2},{7,3},{12,8},{13,9},{14,10},{15,11},{20,16},{21,... | collective-permute-start | bytes 49160 | tf_op jit(solution)/shard_map/ppermute | solution.py:34
  64.4 7.4 %collective-permute-start.7 = (bf16[256,1,32]{0,2,1:T(8,128)(2,1)S(1)}, bf16[256,1,32]{0,2,1:T(8,128)(2,1)S(1)}, u32[]{:S(2)}, u32[]{:S(2)}) collective-permute-start(bf16[256,1,32]{0,2,1:T(8,128)(2,1)S(1)} %get-tuple-element.53), channel_id=1, source_target_pairs={{0,4},{1,5},{2,6},{3,7},{8,12},{9,13},{10,14},{11,15},{16,20},{17,... | collective-permute-start | bytes 49160 | tf_op jit(solution)/shard_map/ppermute | solution.py:31
  67.4 6.4 %collective-permute-start.6 = (bf16[256,1,64]{0,2,1:T(8,128)(2,1)S(1)}, bf16[256,1,64]{0,2,1:T(8,128)(2,1)S(1)}, u32[]{:S(2)}, u32[]{:S(2)}) collective-permute-start(bf16[256,1,64]{0,2,1:T(8,128)(2,1)S(1)} %get-tuple-element.44), channel_id=1, source_target_pairs={{4,0},{5,1},{6,2},{7,3},{12,8},{13,9},{14,10},{15,11},{20,16},{21,... | collective-permute-start | bytes 98312 | tf_op jit(solution)/shard_map/ppermute | solution.py:34
  68.7 5.1 %collective-permute-start.5 = (bf16[256,1,64]{0,2,1:T(8,128)(2,1)S(1)}, bf16[256,1,64]{0,2,1:T(8,128)(2,1)S(1)}, u32[]{:S(2)}, u32[]{:S(2)}) collective-permute-start(bf16[256,1,64]{0,2,1:T(8,128)(2,1)S(1)} %get-tuple-element.43), channel_id=1, source_target_pairs={{0,4},{1,5},{2,6},{3,7},{8,12},{9,13},{10,14},{11,15},{16,20},{17,... | collective-permute-start | bytes 98312 | tf_op jit(solution)/shard_map/ppermute | solution.py:31
  72.9 1.2 copy-start.2
  73.8 3.5 %copy-start.6 = (bf16[64,512]{1,0:T(8,128)(2,1)S(1)}, bf16[64,512]{1,0:T(8,128)(2,1)}, u32[]{:S(2)}) copy-start(bf16[64,512]{1,0:T(8,128)(2,1)} %param.11) | copy-start | bytes 196612
  110.7 4.8 %collective-permute-start.4 = (bf16[256,1,128]{2,1,0:T(2,128)(2,1)S(1)}, bf16[256,1,128]{2,1,0:T(2,128)(2,1)S(1)}, u32[]{:S(2)}, u32[]{:S(2)}) collective-permute-start(bf16[256,1,128]{2,1,0:T(2,128)(2,1)S(1)} %get-tuple-element.31), channel_id=1, source_target_pairs={{4,0},{5,1},{6,2},{7,3},{12,8},{13,9},{14,10},{15,11},{20,16},{21,... | collective-permute-start | bytes 196616 | tf_op jit(solution)/shard_map/ppermute | solution.py:34
  112.0 4.0 %collective-permute-start.3 = (bf16[256,1,128]{2,1,0:T(2,128)(2,1)S(1)}, bf16[256,1,128]{2,1,0:T(2,128)(2,1)S(1)}, u32[]{:S(2)}, u32[]{:S(2)}) collective-permute-start(bf16[256,1,128]{2,1,0:T(2,128)(2,1)S(1)} %get-tuple-element.30), channel_id=1, source_target_pairs={{0,4},{1,5},{2,6},{3,7},{8,12},{9,13},{10,14},{11,15},{16,20},{17,... | collective-permute-start | bytes 196616 | tf_op jit(solution)/shard_map/ppermute | solution.py:31
  118.9 2.2 %copy-start.3 = (bf16[64,9,256]{2,0,1:T(8,128)(2,1)S(1)}, bf16[64,9,256]{2,0,1:T(8,128)(2,1)}, u32[]{:S(2)}) copy-start(bf16[64,9,256]{2,0,1:T(8,128)(2,1)} %get-tuple-element.33) | copy-start | bytes 884740
  122.9 1.2 copy-start.1
  125.3 0.7 copy-start.12
  125.3 0.7 copy-start.13
  125.3 16.1 %copy-start.10 = (f32[64]{0:T(128)S(1)}, f32[64]{0:T(128)}, u32[]{:S(2)}) copy-start(f32[64]{0:T(128)} %get-tuple-element.86) | copy-start | bytes 772
  125.3 16.1 %copy-start.11 = (f32[64]{0:T(128)S(1)}, f32[64]{0:T(128)}, u32[]{:S(2)}) copy-start(f32[64]{0:T(128)} %get-tuple-element.87) | copy-start | bytes 772
  125.3 17.0 %copy-start.8 = (f32[64]{0:T(128)S(1)}, f32[64]{0:T(128)}, u32[]{:S(2)}) copy-start(f32[64]{0:T(128)} %get-tuple-element.82) | copy-start | bytes 772
  125.3 17.0 %copy-start.9 = (f32[64]{0:T(128)S(1)}, f32[64]{0:T(128)}, u32[]{:S(2)}) copy-start(f32[64]{0:T(128)} %get-tuple-element.84) | copy-start | bytes 772
  141.5 2.4 %copy-start.7 = (bf16[64,128]{1,0:T(8,128)(2,1)}, bf16[64,128]{1,0:T(8,128)(2,1)S(1)}, u32[]{:S(2)}) copy-start(bf16[64,128]{1,0:T(8,128)(2,1)S(1)} %fusion.81) | copy-start | bytes 49156
Sparse Core Ops, SparseCore 0:
  41.9 35.2 all-gather.2
  80.5 26.4 all-gather.4
